TPU v7x, 32 devices: a whole 2x2x4 slice. The times are simulated.
32 devices in a mesh: layer: 16 (over z, x, core), dp: 2 (over y).
Axes of the slice: x: 2, y: 2, z: 4, core: 2. Of those that a mesh axis runs over, the one named last changes fastest.
Arguments:
- weights: float32 [32, 1024, 1024], P('layer', 'dp'), may hold values from -6 to 6
- momentum: float32 [32, 1024, 1024], P('layer', 'dp'), may hold values from -3 to 3
- boundary: float32 [16, 512, 1024], P('layer', 'dp'), may hold values from -6 to 6
- adjoint: float32 [16, 512, 1024], P('layer', 'dp'), may hold values from -6 to 6
- target: float32 [512, 1024], P('dp'), may hold values from -6 to 6
Outputs:
- new_weights: float32 [32, 1024, 1024], P('layer', 'dp')
- new_momentum: float32 [32, 1024, 1024], P('layer', 'dp')
- new_boundary: float32 [16, 512, 1024], P('layer', 'dp')
- new_adjoint: float32 [16, 512, 1024], P('layer', 'dp')
All inputs are finite; a program needn't handle non-finite values.
Results may differ from a plain program's by a relative error of at most 0.012.
Values may be sent and summed in bfloat16 or wider, within the bound.
A program may use at most 64 MiB of HBM per device.

v0:
```python
import math
import jax
import jax.numpy as jnp
from jax import lax
from jax.sharding import PartitionSpec as P

STEPS = 2
SWEEPS = 2
step_size = 0.5
momentum_decay = 0.9
learn_rate = 0.05


def passed_along(value, axis, by):
    devices = lax.axis_size(axis)
    pairs = [(i, i + by) for i in range(devices) if 0 <= i + by < devices]
    return lax.ppermute(value, axis, pairs)


def forward_group(current, full_weights, width_scale):
    inputs_list = []
    slopes_list = []
    for layer_at in range(full_weights.shape[0]):
        rounded = current.astype(jnp.bfloat16)
        product = jnp.dot(rounded, full_weights[layer_at], preferred_element_type=jnp.float32)
        squashed = jnp.tanh(product * width_scale)
        current = current + step_size * squashed
        inputs_list.append(rounded)
        slopes_list.append(squashed)
    return (current, inputs_list, slopes_list)


def pull_back(signal, matrix):
    return lax.dot_general(
        signal, matrix, (((1,), (1,)), ((), ())), preferred_element_type=jnp.float32
    )


def backward_group(cotangent, full_weights, slopes_list, width_scale):
    for layer_at in reversed(range(len(slopes_list))):
        slope = slopes_list[layer_at]
        signal = (cotangent * (1.0 - slope * slope)).astype(jnp.bfloat16)
        cotangent = cotangent + step_size * width_scale * pull_back(signal, full_weights[layer_at])
    return cotangent


def outer_rows(left, right):
    return lax.dot_general(
        left, right, (((0,), (0,)), ((), ())), preferred_element_type=jnp.float32
    )


def local(weights, momentum, boundary, adjoint, target):
    groups = lax.axis_size("layer")
    group_at = lax.axis_index("layer")
    shards = lax.axis_size("dp")
    shard_at = lax.axis_index("dp")
    width = weights.shape[2]
    own_rows = weights.shape[1]
    width_scale = 1.0 / math.sqrt(width)
    row_scale = 1.0 / math.sqrt(boundary.shape[1] * shards)
    is_first = group_at == 0
    is_last = group_at == groups - 1
    current_in = boundary[0]
    cotangent_in = adjoint[0]
    for update_at in range(STEPS):
        full_weights = lax.all_gather(weights.astype(jnp.bfloat16), "dp", axis=1, tiled=True)
        for sweep_at in range(SWEEPS):
            outgoing = forward_group(current_in, full_weights, width_scale)[0]
            received = passed_along(outgoing, "layer", 1)
            current_in = jnp.where(is_first, current_in, received)
        finals, inputs_list, slopes_list = forward_group(current_in, full_weights, width_scale)
        missing = finals - target
        for sweep_at in range(SWEEPS):
            starting = backward_group(cotangent_in, full_weights, slopes_list, width_scale)
            received = passed_along(starting, "layer", -1)
            cotangent_in = jnp.where(is_last, missing, received)
        cotangent = cotangent_in
        grads = [None] * len(slopes_list)
        for layer_at in reversed(range(len(slopes_list))):
            slope = slopes_list[layer_at]
            signal = (cotangent * (1.0 - slope * slope)).astype(jnp.bfloat16)
            layer_input = inputs_list[layer_at]
            columns = lax.dynamic_slice_in_dim(
                lax.all_gather(layer_input, "dp", axis=0, tiled=True),
                shard_at * own_rows,
                own_rows,
                1,
            )
            summed = outer_rows(columns, lax.all_gather(signal, "dp", axis=0, tiled=True))
            grads[layer_at] = summed * row_scale
            if layer_at > 0:
                cotangent = cotangent + step_size * width_scale * pull_back(
                    signal, full_weights[layer_at]
                )
        momentum = momentum_decay * momentum + jnp.stack(grads, axis=0)
        weights = weights - learn_rate * momentum
    return (weights, momentum, current_in[None], cotangent_in[None])


def solution(mesh):
    placed = (
        P("layer", "dp", None),
        P("layer", "dp", None),
        P("layer", "dp", None),
        P("layer", "dp", None),
        P("dp", None),
    )
    return jax.shard_map(
        local,
        mesh=mesh,
        in_specs=placed,
        out_specs=(
            P("layer", "dp", None),
            P("layer", "dp", None),
            P("layer", "dp", None),
            P("layer", "dp", None),
        ),
        check_vma=False,
    )
```

profile of v0, /device:TPU:0, one launch (start us, length us, event | category | flops | bytes accessed | tf_op | source)
XLA Modules:
  0.0 482.2 jit_solution(8640510637645091248)
XLA Ops:
  7.2 3.9 convert_element_type.81
  11.2 59.6 %all-gather.11.cloned.1.call-done = bf16[2,1024,1024]{2,1,0:T(8,128)(2,1)} async-done(((bf16[2,512,1024]{2,1,0:T(8,128)(2,1)}), bf16[2,1024,1024]{2,1,0:T(8,128)(2,1)}) %all-gather.11.cloned.1.call-update) | async-done | bytes 4194320 | tf_op jit(solution)/shard_map/all_gather | solution.py:67
  70.8 2.5 fusion.40
  73.2 0.3 copy-done
  73.6 0.7 fusion.37
  74.3 1.6 collective-permute-start
  76.0 2.2 collective-permute-done
  78.2 2.8 fusion.34
  81.0 0.8 fusion.31
  81.7 13.3 %collective-permute-start.1 = (f32[256,1024]{1,0:T(8,128)S(1)}, f32[256,1024]{1,0:T(8,128)S(1)}, u32[]{:S(2)}, u32[]{:S(2)}) collective-permute-start(f32[256,1024]{1,0:T(8,128)S(1)} %fusion.31), channel_id=1, source_target_pairs={{0,2},{2,4},{4,6},{6,8},{8,10},{10,12},{12,14},{14,16},{16,18},{18... | collective-permute-start | bytes 3145736 | tf_op jit(solution)/shard_map/ppermute | solution.py:17
  95.1 2.2 collective-permute-done.1
  97.6 3.3 fusion.69
  101.0 3.0 add_subtract_fusion.1
  104.5 0.7 fusion.26
  105.3 1.8 fusion.25
  107.1 1.3 collective-permute-start.2
  108.4 16.2 %collective-permute-done.2 = f32[256,1024]{1,0:T(8,128)} collective-permute-done((f32[256,1024]{1,0:T(8,128)}, f32[256,1024]{1,0:T(8,128)}, u32[]{:S(2)}, u32[]{:S(2)}) %collective-permute-start.2) | collective-permute-done | bytes 1048608 | tf_op jit(solution)/shard_map/ppermute | solution.py:17
  124.6 3.3 fusion.24
  127.9 1.8 fusion.23
  129.7 1.3 collective-permute-start.3
  131.0 15.8 %collective-permute-done.3 = f32[256,1024]{1,0:T(8,128)} collective-permute-done((f32[256,1024]{1,0:T(8,128)}, f32[256,1024]{1,0:T(8,128)}, u32[]{:S(2)}, u32[]{:S(2)}) %collective-permute-start.3) | collective-permute-done | bytes 1048608 | tf_op jit(solution)/shard_map/ppermute | solution.py:17
  146.8 2.7 multiply_convert_fusion.9
  149.5 3.7 fusion.41
  153.3 0.5 all-gather.17.cloned.1.call-update
  153.8 0.5 all-gather.19.cloned.1.call-update
  154.6 13.2 %all-gather.13.cloned.1.call-done = bf16[512,1024]{1,0:T(8,128)(2,1)} async-done(((bf16[256,1024]{1,0:T(8,128)(2,1)}), bf16[512,1024]{1,0:T(8,128)(2,1)}) %all-gather.13.cloned.1.call-update) | async-done | bytes 1048592 | tf_op jit(solution)/shard_map/all_gather | solution.py:85
  167.8 23.4 %all-gather.15.cloned.1.call-done = bf16[512,1024]{1,0:T(8,128)(2,1)} async-done(((bf16[256,1024]{1,0:T(8,128)(2,1)}), bf16[512,1024]{1,0:T(8,128)(2,1)}) %all-gather.15.cloned.1.call-update) | async-done | bytes 1048592 | tf_op jit(solution)/shard_map/all_gather | solution.py:90
  191.2 3.4 multiply_bitcast_fusion.3
  194.6 19.9 %all-gather.17.cloned.1.call-done = bf16[512,1024]{1,0:T(8,128)(2,1)} async-done(((bf16[256,1024]{1,0:T(8,128)(2,1)}), bf16[512,1024]{1,0:T(8,128)(2,1)}) %all-gather.17.cloned.1.call-update) | async-done | bytes 1048592 | tf_op jit(solution)/shard_map/all_gather | solution.py:85
  214.5 23.3 %all-gather.19.cloned.1.call-done = bf16[512,1024]{1,0:T(8,128)(2,1)} async-done(((bf16[256,1024]{1,0:T(8,128)(2,1)}), bf16[512,1024]{1,0:T(8,128)(2,1)}) %all-gather.19.cloned.1.call-update) | async-done | bytes 1048592 | tf_op jit(solution)/shard_map/all_gather | solution.py:90
  237.8 2.3 multiply_bitcast_fusion.2
  240.1 1.4 copy-done.13
  241.4 5.8 %fusion = bf16[2,512,1024]{2,1,0:T(8,128)(2,1)} fusion(f32[2,512,1024]{2,1,0:T(8,128)S(1)} %copy-done.6, f32[1,512,1024]{2,1,0:T(8,128)S(1)} %multiply_bitcast_fusion.2, f32[1,512,1024]{2,1,0:T(8,128)} %multiply_bitcast_fusion.3, f32[2,512,1024]{2,1,0:T(8,128)} %param.6), kind=kLoop, calls=%fused_computation.12 | loop fusion | flops 6291456 | bytes 14680064 | tf_op jit(solution)/shard_map/convert_element_type | solution.py:67
  247.3 56.8 %all-gather.21.cloned.1.call-done = bf16[2,1024,1024]{2,1,0:T(8,128)(2,1)} async-done(((bf16[2,512,1024]{2,1,0:T(8,128)(2,1)}), bf16[2,1024,1024]{2,1,0:T(8,128)(2,1)}) %all-gather.21.cloned.1.call-update) | async-done | bytes 4194320 | tf_op jit(solution)/shard_map/all_gather | solution.py:67
  304.1 2.5 fusion.20
  307.0 0.8 fusion.17
  307.7 1.6 collective-permute-start.4
  309.4 2.2 collective-permute-done.4
  311.6 0.9 fusion.14
  312.5 0.8 fusion.11
  313.2 13.3 %collective-permute-start.5 = (f32[256,1024]{1,0:T(8,128)S(1)}, f32[256,1024]{1,0:T(8,128)S(1)}, u32[]{:S(2)}, u32[]{:S(2)}) collective-permute-start(f32[256,1024]{1,0:T(8,128)S(1)} %fusion.11), channel_id=1, source_target_pairs={{0,2},{2,4},{4,6},{6,8},{8,10},{10,12},{12,14},{14,16},{16,18},{18... | collective-permute-start | bytes 3145736 | tf_op jit(solution)/shard_map/ppermute | solution.py:17
  326.6 2.2 collective-permute-done.5
  328.8 1.1 fusion.84
  329.9 3.7 fusion.70
  333.6 3.3 add_subtract_fusion
  337.2 2.5 fusion.6
  339.6 0.8 fusion.5
  340.4 1.3 collective-permute-start.6
  341.7 14.7 %collective-permute-done.6 = f32[256,1024]{1,0:T(8,128)S(1)} collective-permute-done((f32[256,1024]{1,0:T(8,128)S(1)}, f32[256,1024]{1,0:T(8,128)S(1)}, u32[]{:S(2)}, u32[]{:S(2)}) %collective-permute-start.6) | collective-permute-done | bytes 1048608 | tf_op jit(solution)/shard_map/ppermute | solution.py:17
  356.4 0.9 fusion.4
  357.3 1.8 fusion.3
  359.1 1.3 collective-permute-start.7
  360.4 15.8 %collective-permute-done.7 = f32[256,1024]{1,0:T(8,128)} collective-permute-done((f32[256,1024]{1,0:T(8,128)}, f32[256,1024]{1,0:T(8,128)}, u32[]{:S(2)}, u32[]{:S(2)}) %collective-permute-start.7) | collective-permute-done | bytes 1048608 | tf_op jit(solution)/shard_map/ppermute | solution.py:17
  376.3 2.7 fusion.71
  379.0 3.7 fusion.42
  382.8 0.7 all-gather.27.cloned.1.call-update
  384.1 13.1 %all-gather.23.cloned.1.call-done = bf16[512,1024]{1,0:T(8,128)(2,1)} async-done(((bf16[256,1024]{1,0:T(8,128)(2,1)}), bf16[512,1024]{1,0:T(8,128)(2,1)}) %all-gather.23.cloned.1.call-update) | async-done | bytes 1048592 | tf_op jit(solution)/shard_map/all_gather | solution.py:85
  397.2 22.9 %all-gather.25.cloned.1.call-done = bf16[512,1024]{1,0:T(8,128)(2,1)} async-done(((bf16[256,1024]{1,0:T(8,128)(2,1)}), bf16[512,1024]{1,0:T(8,128)(2,1)}) %all-gather.25.cloned.1.call-update) | async-done | bytes 1048592 | tf_op jit(solution)/shard_map/all_gather | solution.py:90
  420.1 3.5 multiply_bitcast_fusion.1
  423.5 19.4 %all-gather.27.cloned.1.call-done = bf16[512,1024]{1,0:T(8,128)(2,1)} async-done(((bf16[256,1024]{1,0:T(8,128)(2,1)}), bf16[512,1024]{1,0:T(8,128)(2,1)}) %all-gather.27.cloned.1.call-update) | async-done | bytes 1048592 | tf_op jit(solution)/shard_map/all_gather | solution.py:85
  442.9 23.3 %all-gather.29.cloned.1.call-done = bf16[512,1024]{1,0:T(8,128)(2,1)} async-done(((bf16[256,1024]{1,0:T(8,128)(2,1)}), bf16[512,1024]{1,0:T(8,128)(2,1)}) %all-gather.29.cloned.1.call-update) | async-done | bytes 1048592 | tf_op jit(solution)/shard_map/all_gather | solution.py:90
  466.2 2.3 multiply_bitcast_fusion
  468.5 0.4 copy-done.7
  468.9 6.5 %multiply_subtract_fusion = (f32[2,512,1024]{2,1,0:T(8,128)}, f32[2,512,1024]{2,1,0:T(8,128)}) fusion(f32[2,512,1024]{2,1,0:T(8,128)S(1)} %copy-done.7, f32[1,512,1024]{2,1,0:T(8,128)} %copy-done.13, f32[1,512,1024]{2,1,0:T(8,128)S(1)} %copy-done.12, f32[2,512,1024]{2,1,0:T(8,128)} %param.6, f32[1,512,1024]{2,1,0:T(8,128)S(1)} %multiply_bitcast_fusion, ...), kind=kLoop, calls=%fused_computation.2 | loop fusion | flops 10485760 | bytes 25165824 | tf_op jit(solution)/shard_map/sub | solution.py:97
  (53 shorter events, 2.8 us)
Async XLA Ops:
  7.2 63.6 %copy-start.16 = (f32[1,256,1024]{2,1,0:T(8,128)S(1)}, f32[1,256,1024]{2,1,0:T(8,128)}, u32[]{:S(2)}) copy-start(f32[1,256,1024]{2,1,0:T(8,128)} %param.7) | copy-start | bytes 3145732
  7.2 63.6 %all-gather.11.cloned.1.call-start = ((), (), s32[]{:S(2)}) async-start(), calls=%async_computation | async-start | bytes 6291456 | tf_op jit(solution)/shard_map/all_gather | solution.py:67
  11.2 156.6 %all-gather.13.cloned.1.call-start = ((), (), s32[]{:S(2)}) async-start(), calls=%async_computation.1 | async-start | bytes 1572864 | tf_op jit(solution)/shard_map/all_gather | solution.py:85
  70.8 2.8 copy-start
  74.3 3.9 collective-permute-start
  76.0 5.0 %copy-start.1 = (bf16[2,1024,1024]{2,1,0:T(8,128)(2,1)S(1)}, bf16[2,1024,1024]{2,1,0:T(8,128)(2,1)}, u32[]{:S(2)}) copy-start(bf16[2,1024,1024]{2,1,0:T(8,128)(2,1)} %all-gather.11.cloned.1.call-done) | copy-start | bytes 12582916
  78.2 3.6 copy-start.18
  81.7 15.5 %collective-permute-start.1 = (f32[256,1024]{1,0:T(8,128)S(1)}, f32[256,1024]{1,0:T(8,128)S(1)}, u32[]{:S(2)}, u32[]{:S(2)}) collective-permute-start(f32[256,1024]{1,0:T(8,128)S(1)} %fusion.31), channel_id=1, source_target_pairs={{0,2},{2,4},{4,6},{6,8},{8,10},{10,12},{12,14},{14,16},{16,18},{18... | collective-permute-start | bytes 3145736 | tf_op jit(solution)/shard_map/ppermute | solution.py:17
  97.6 3.3 copy-start.14
  101.0 3.3 copy-start.2
  101.0 3.6 copy-start.17
  104.0 3.1 copy-start.10
  107.1 17.6 %collective-permute-start.2 = (f32[256,1024]{1,0:T(8,128)}, f32[256,1024]{1,0:T(8,128)}, u32[]{:S(2)}, u32[]{:S(2)}) collective-permute-start(f32[256,1024]{1,0:T(8,128)} %fusion.25), channel_id=1, source_target_pairs={{2,0},{4,2},{6,4},{8,6},{10,8},{12,10},{14,12},{16,14},{18,16},{20... | collective-permute-start | bytes 3145736 | tf_op jit(solution)/shard_map/ppermute | solution.py:17
  108.4 19.5 %copy-start.3 = (bf16[2,1024,1024]{2,1,0:T(8,128)(2,1)S(1)}, bf16[2,1024,1024]{2,1,0:T(8,128)(2,1)}, u32[]{:S(2)}) copy-start(bf16[2,1024,1024]{2,1,0:T(8,128)(2,1)} %all-gather.11.cloned.1.call-done) | copy-start | bytes 12582916
  129.7 17.2 %collective-permute-start.3 = (f32[256,1024]{1,0:T(8,128)}, f32[256,1024]{1,0:T(8,128)}, u32[]{:S(2)}, u32[]{:S(2)}) collective-permute-start(f32[256,1024]{1,0:T(8,128)} %fusion.23), channel_id=1, source_target_pairs={{2,0},{4,2},{6,4},{8,6},{10,8},{12,10},{14,12},{16,14},{18,16},{20... | collective-permute-start | bytes 3145736 | tf_op jit(solution)/shard_map/ppermute | solution.py:17
  131.0 60.2 %all-gather.15.cloned.1.call-start = ((), (), s32[]{:S(2)}) async-start(), calls=%async_computation.2 | async-start | bytes 1572864 | tf_op jit(solution)/shard_map/all_gather | solution.py:90
  153.2 61.3 %all-gather.17.cloned.1.call-start = ((), (), s32[]{:S(2)}) async-start(), calls=%async_computation.3 | async-start | bytes 1572864 | tf_op jit(solution)/shard_map/all_gather | solution.py:85
  153.8 84.0 %all-gather.19.cloned.1.call-start = ((), (), s32[]{:S(2)}) async-start(), calls=%async_computation.4 | async-start | bytes 1572864 | tf_op jit(solution)/shard_map/all_gather | solution.py:90
  154.4 149.8 %all-gather.21.cloned.1.call-start = ((), (), s32[]{:S(2)}) async-start(), calls=%async_computation.5 | async-start | bytes 6291456 | tf_op jit(solution)/shard_map/all_gather | solution.py:67
  237.8 3.6 copy-start.6
  240.0 1.4 copy-start.13
  241.4 62.7 %copy-start.15 = (bf16[256,1024]{1,0:T(8,128)(2,1)S(1)}, bf16[256,1024]{1,0:T(8,128)(2,1)}, u32[]{:S(2)}) copy-start(bf16[256,1024]{1,0:T(8,128)(2,1)} %copy-done.14) | copy-start | bytes 1572868
  247.3 149.9 %all-gather.23.cloned.1.call-start = ((), (), s32[]{:S(2)}) async-start(), calls=%async_computation.6 | async-start | bytes 1572864 | tf_op jit(solution)/shard_map/all_gather | solution.py:85
  304.1 2.8 copy-start.4
  307.7 3.9 collective-permute-start.4
  313.2 15.6 %collective-permute-start.5 = (f32[256,1024]{1,0:T(8,128)S(1)}, f32[256,1024]{1,0:T(8,128)S(1)}, u32[]{:S(2)}, u32[]{:S(2)}) collective-permute-start(f32[256,1024]{1,0:T(8,128)S(1)} %fusion.11), channel_id=1, source_target_pairs={{0,2},{2,4},{4,6},{6,8},{8,10},{10,12},{12,14},{14,16},{16,18},{18... | collective-permute-start | bytes 3145736 | tf_op jit(solution)/shard_map/ppermute | solution.py:17
  329.9 3.7 copy-start.11
  333.6 3.6 copy-start.5
  336.9 19.6 %copy-start.8 = (f32[256,1024]{1,0:T(8,128)}, f32[256,1024]{1,0:T(8,128)S(1)}, u32[]{:S(2)}) copy-start(f32[256,1024]{1,0:T(8,128)S(1)} %get-tuple-element.19) | copy-start | bytes 3145732
  340.4 16.0 %collective-permute-start.6 = (f32[256,1024]{1,0:T(8,128)S(1)}, f32[256,1024]{1,0:T(8,128)S(1)}, u32[]{:S(2)}, u32[]{:S(2)}) collective-permute-start(f32[256,1024]{1,0:T(8,128)S(1)} %fusion.5), channel_id=1, source_target_pairs={{2,0},{4,2},{6,4},{8,6},{10,8},{12,10},{14,12},{16,14},{18,16},{20... | collective-permute-start | bytes 3145736 | tf_op jit(solution)/shard_map/ppermute | solution.py:17
  357.3 19.0 %copy-start.9 = (f32[256,1024]{1,0:T(8,128)S(1)}, f32[256,1024]{1,0:T(8,128)}, u32[]{:S(2)}) copy-start(f32[256,1024]{1,0:T(8,128)} %copy-done.8) | copy-start | bytes 3145732
  359.1 17.2 %collective-permute-start.7 = (f32[256,1024]{1,0:T(8,128)}, f32[256,1024]{1,0:T(8,128)}, u32[]{:S(2)}, u32[]{:S(2)}) collective-permute-start(f32[256,1024]{1,0:T(8,128)} %fusion.3), channel_id=1, source_target_pairs={{2,0},{4,2},{6,4},{8,6},{10,8},{12,10},{14,12},{16,14},{18,16},{20... | collective-permute-start | bytes 3145736 | tf_op jit(solution)/shard_map/ppermute | solution.py:17
  360.4 59.7 %all-gather.25.cloned.1.call-start = ((), (), s32[]{:S(2)}) async-start(), calls=%async_computation.7 | async-start | bytes 1572864 | tf_op jit(solution)/shard_map/all_gather | solution.py:90
  382.7 60.2 %all-gather.27.cloned.1.call-start = ((), (), s32[]{:S(2)}) async-start(), calls=%async_computation.8 | async-start | bytes 1572864 | tf_op jit(solution)/shard_map/all_gather | solution.py:85
  383.5 82.7 %all-gather.29.cloned.1.call-start = ((), (), s32[]{:S(2)}) async-start(), calls=%async_computation.9 | async-start | bytes 1572864 | tf_op jit(solution)/shard_map/all_gather | solution.py:90
  384.1 84.4 %copy-start.12 = (f32[1,512,1024]{2,1,0:T(8,128)S(1)}, f32[1,512,1024]{2,1,0:T(8,128)}, u32[]{:S(2)}) copy-start(f32[1,512,1024]{2,1,0:T(8,128)} %multiply_bitcast_fusion.3) | copy-start | bytes 6291460
  466.2 2.7 copy-start.7
Sparse Core Ops, SparseCore 0:
  11.3 59.4 all-gather.10
  131.1 36.6 all-gather.12
  169.9 21.2 all-gather.14
  193.2 21.2 all-gather.16
  216.5 21.2 all-gather.18
  247.4 56.7 all-gather.20
  360.5 36.6 all-gather.22
  398.8 21.2 all-gather.24
  421.6 21.2 all-gather.26
  444.9 21.2 all-gather.28
where the time goes:
time: 483 us; the launch traced here: 482 us
  waiting for transfers between devices  348 us (72%)
  matrix products  57.1 us (12%)
  starting transfers between devices  35.9 us (7%)
  other arithmetic  23.1 us (5%)
  between operations  14.5 us (3%)
    all_gather x2, waiting for transfers between devices, local(): lax.all_gather(weights.astype(jnp.bfloat16), 'dp', axis=1, tiled=True)  116 us
    all_gather x4, waiting for transfers between devices, local(): lax.all_gather(signal, 'dp', axis=0, tiled=True)  92.9 us
    ppermute x8, waiting for transfers between devices, passed_along(): return lax.ppermute(value, axis, pairs)  71.4 us
    all_gather x4, waiting for transfers between devices, local(): lax.all_gather(layer_input, 'dp', axis=0, tiled=True)  65.5 us
    ppermute x8, starting transfers between devices, passed_along(): return lax.ppermute(value, axis, pairs)  35.1 us
    dot_general x12, matrix products, forward_group(): jnp.dot(rounded, full_weights[layer_at], preferred_element_type=jnp.float32)  24.8 us
    dot_general x10, matrix products, pull_back(): lax.dot_general(signal, matrix, (((1,), (1,)), ((), ())), preferred_eleme...  20.8 us
    dot_general x4, matrix products, outer_rows(): lax.dot_general(left, right, (((0,), (0,)), ((), ())), preferred_element_...  11.4 us
  transfers between devices with their start and end apart: 18, of which 18 were waited for; matrix products, arithmetic and copies ran while one was open for 4% of the time, Pallas kernels for 0%

commit v1 on v0

--- a/solution.py
+++ b/solution.py
@@ -9,6 +9,28 @@
 step_size = 0.5
 momentum_decay = 0.9
 learn_rate = 0.05
+
+
+def joined_along(pieces, dim):
+    shape = list(pieces.shape[1:])
+    shape[dim] *= pieces.shape[0]
+    return jnp.moveaxis(pieces, 0, dim).reshape(shape)
+
+
+def grow_blocks(x, axis):
+    devices = lax.axis_size(axis)
+    blocks = x[None]
+    for level in range(devices.bit_length() - 1):
+        stride = 1 << level
+        theirs = lax.ppermute(blocks, axis, [(i, i ^ stride) for i in range(devices)])
+        both = jnp.stack([blocks, theirs])
+        upper = lax.axis_index(axis) >> level & 1
+        blocks = jnp.where(upper == 0, both, both[::-1]).reshape(-1, *x.shape)
+    return blocks
+
+
+def gather_by_bits(x, axis, dim):
+    return joined_along(grow_blocks(x, axis), dim)
 
 
 def passed_along(value, axis, by):
@@ -87,7 +109,7 @@
                 own_rows,
                 1,
             )
-            summed = outer_rows(columns, lax.all_gather(signal, "dp", axis=0, tiled=True))
+            summed = outer_rows(columns, gather_by_bits(signal, "dp", 0))
             grads[layer_at] = summed * row_scale
             if layer_at > 0:
                 cotangent = cotangent + step_size * width_scale * pull_back(

time: 483 us -> 409 us (0.85)
  waiting for transfers between devices: 348 us -> 262 us
  other arithmetic: 23.1 us -> 30.9 us
    all_gather x4 -> x0, waiting for transfers between devices: 92.9 us -> none  [local(): lax.all_gather(signal, 'dp', axis=0, tiled=True)]
    ppermute x0 -> x4, waiting for transfers between devices: none -> 50.5 us  [grow_blocks(): lax.ppermute(blocks, axis, [(i, i ^ stride) for i in range(devices)])]
    all_gather x4, waiting for transfers between devices: 65.5 us -> 23.1 us  [local(): lax.all_gather(layer_input, 'dp', axis=0, tiled=True)]
  transfers between devices with their start and end apart: 18 -> 18, of which waited for: 18 -> 16; matrix products, arithmetic and copies ran while one was open for 4% -> 6% of each run, Pallas kernels for 0% -> 0%
where the time goes in v1:
time: 409 us; the launch traced here: 407 us
  waiting for transfers between devices  262 us (64%)
  matrix products  55.4 us (14%)
  starting transfers between devices  39.9 us (10%)
  other arithmetic  30.9 us (8%)
  between operations  14.5 us (4%)
  local copies, waits for them, and re-layouts  4.14 us (1%)
    all_gather x2, waiting for transfers between devices, local(): lax.all_gather(weights.astype(jnp.bfloat16), 'dp', axis=1, tiled=True)  117 us
    ppermute x8, waiting for transfers between devices, passed_along(): return lax.ppermute(value, axis, pairs)  71.1 us
    ppermute x4, waiting for transfers between devices, grow_blocks(): lax.ppermute(blocks, axis, [(i, i ^ stride) for i in range(devices)])  50.5 us
    ppermute x8, starting transfers between devices, passed_along(): return lax.ppermute(value, axis, pairs)  35.1 us
    dot_general x12, matrix products, forward_group(): jnp.dot(rounded, full_weights[layer_at], preferred_element_type=jnp.float32)  24.8 us
    all_gather x4, waiting for transfers between devices, local(): lax.all_gather(layer_input, 'dp', axis=0, tiled=True)  23.1 us
    dot_general x10, matrix products, pull_back(): lax.dot_general(signal, matrix, (((1,), (1,)), ((), ())), preferred_eleme...  19.4 us
    dot_general x4, matrix products, outer_rows(): lax.dot_general(left, right, (((0,), (0,)), ((), ())), preferred_element_...  11.2 us
  transfers between devices with their start and end apart: 18, of which 16 were waited for; matrix products, arithmetic and copies ran while one was open for 6% of the time, Pallas kernels for 0%

profile of v1, /device:TPU:0, one launch (start us, length us, event | category | flops | bytes accessed | tf_op | source)
XLA Modules:
  0.0 407.0 jit_solution(9841727404903846296)
XLA Ops:
  7.2 3.9 convert_element_type.81
  11.2 59.6 %all-gather.7.cloned.1.call-done = bf16[2,1024,1024]{2,1,0:T(8,128)(2,1)} async-done(((bf16[2,512,1024]{2,1,0:T(8,128)(2,1)}), bf16[2,1024,1024]{2,1,0:T(8,128)(2,1)}) %all-gather.7.cloned.1.call-update) | async-done | bytes 4194320 | tf_op jit(solution)/shard_map/all_gather | solution.py:89
  70.8 2.5 fusion.40
  74.3 1.6 collective-permute-start
  76.0 2.2 collective-permute-done
  78.2 2.8 fusion.34
  81.0 0.8 fusion.31
  81.7 13.3 %collective-permute-start.1 = (f32[256,1024]{1,0:T(8,128)S(1)}, f32[256,1024]{1,0:T(8,128)S(1)}, u32[]{:S(2)}, u32[]{:S(2)}) collective-permute-start(f32[256,1024]{1,0:T(8,128)S(1)} %fusion.31), channel_id=1, source_target_pairs={{0,2},{2,4},{4,6},{6,8},{8,10},{10,12},{12,14},{14,16},{16,18},{18... | collective-permute-start | bytes 3145736 | tf_op jit(solution)/shard_map/ppermute | solution.py:39
  95.1 2.2 collective-permute-done.1
  97.6 3.3 fusion.69
  101.0 3.0 add_subtract_fusion.1
  105.3 1.8 fusion.25
  107.1 1.3 collective-permute-start.2
  108.4 16.2 %collective-permute-done.2 = f32[256,1024]{1,0:T(8,128)} collective-permute-done((f32[256,1024]{1,0:T(8,128)}, f32[256,1024]{1,0:T(8,128)}, u32[]{:S(2)}, u32[]{:S(2)}) %collective-permute-start.2) | collective-permute-done | bytes 1048608 | tf_op jit(solution)/shard_map/ppermute | solution.py:39
  124.6 3.3 fusion.24
  127.9 1.8 fusion.23
  129.7 1.3 collective-permute-start.3
  131.0 15.8 %collective-permute-done.3 = f32[256,1024]{1,0:T(8,128)} collective-permute-done((f32[256,1024]{1,0:T(8,128)}, f32[256,1024]{1,0:T(8,128)}, u32[]{:S(2)}, u32[]{:S(2)}) %collective-permute-start.3) | collective-permute-done | bytes 1048608 | tf_op jit(solution)/shard_map/ppermute | solution.py:39
  146.8 2.7 multiply_convert_fusion.9
  150.1 3.7 fusion.41
  153.8 1.5 collective-permute-start.4
  155.5 8.7 %collective-permute-done.5 = bf16[1,256,1024]{2,1,0:T(8,128)(2,1)} collective-permute-done((bf16[1,256,1024]{2,1,0:T(8,128)(2,1)}, bf16[1,256,1024]{2,1,0:T(8,128)(2,1)}, u32[]{:S(2)}, u32[]{:S(2)}) %collective-permute-start.5) | collective-permute-done | bytes 524320 | tf_op jit(solution)/shard_map/ppermute | solution.py:25
  164.1 1.3 pad_maximum_fusion.1
  165.4 15.7 %collective-permute-done.4 = bf16[1,256,1024]{2,1,0:T(8,128)(2,1)S(1)} collective-permute-done((bf16[1,256,1024]{2,1,0:T(8,128)(2,1)}, bf16[1,256,1024]{2,1,0:T(8,128)(2,1)S(1)}, u32[]{:S(2)}, u32[]{:S(2)}) %collective-permute-start.4) | collective-permute-done | bytes 524320 | tf_op jit(solution)/shard_map/ppermute | solution.py:25
  181.2 0.8 copy-done.20
  182.0 1.3 pad_maximum_fusion
  183.3 1.2 reverse_select_fusion.2
  184.5 3.5 multiply_bitcast_fusion.2
  188.1 1.2 reverse_select_fusion.3
  189.3 10.4 %all-gather.9.cloned.1.call-done = bf16[512,1024]{1,0:T(8,128)(2,1)} async-done(((bf16[256,1024]{1,0:T(8,128)(2,1)}), bf16[512,1024]{1,0:T(8,128)(2,1)}) %all-gather.9.cloned.1.call-update) | async-done | bytes 1048592 | tf_op jit(solution)/shard_map/all_gather | solution.py:107
  199.6 2.3 multiply_bitcast_fusion.3
  201.9 1.3 copy-done.14
  203.3 5.8 %fusion = bf16[2,512,1024]{2,1,0:T(8,128)(2,1)} fusion(f32[2,512,1024]{2,1,0:T(8,128)S(1)} %copy-done.7, f32[1,512,1024]{2,1,0:T(8,128)} %multiply_bitcast_fusion.2, f32[1,512,1024]{2,1,0:T(8,128)S(1)} %multiply_bitcast_fusion.3, f32[2,512,1024]{2,1,0:T(8,128)} %param.6), kind=kLoop, calls=%fused_computation.12 | loop fusion | flops 6291456 | bytes 14680064 | tf_op jit(solution)/shard_map/convert_element_type | solution.py:89
  209.2 57.8 %all-gather.13.cloned.1.call-done = bf16[2,1024,1024]{2,1,0:T(8,128)(2,1)} async-done(((bf16[2,512,1024]{2,1,0:T(8,128)(2,1)}), bf16[2,1024,1024]{2,1,0:T(8,128)(2,1)}) %all-gather.13.cloned.1.call-update) | async-done | bytes 4194320 | tf_op jit(solution)/shard_map/all_gather | solution.py:89
  266.9 2.5 fusion.20
  269.7 0.8 fusion.17
  270.5 1.6 collective-permute-start.6
  272.2 2.2 collective-permute-done.6
  274.4 0.9 fusion.14
  275.2 0.8 fusion.11
  276.0 13.3 %collective-permute-start.7 = (f32[256,1024]{1,0:T(8,128)S(1)}, f32[256,1024]{1,0:T(8,128)S(1)}, u32[]{:S(2)}, u32[]{:S(2)}) collective-permute-start(f32[256,1024]{1,0:T(8,128)S(1)} %fusion.11), channel_id=1, source_target_pairs={{0,2},{2,4},{4,6},{6,8},{8,10},{10,12},{12,14},{14,16},{16,18},{18... | collective-permute-start | bytes 3145736 | tf_op jit(solution)/shard_map/ppermute | solution.py:39
  289.3 2.2 collective-permute-done.7
  291.6 1.1 fusion.84
  292.7 3.7 fusion.70
  296.3 3.3 add_subtract_fusion
  299.9 2.5 fusion.6
  302.4 0.8 fusion.5
  303.2 1.3 collective-permute-start.8
  304.5 14.7 %collective-permute-done.8 = f32[256,1024]{1,0:T(8,128)S(1)} collective-permute-done((f32[256,1024]{1,0:T(8,128)S(1)}, f32[256,1024]{1,0:T(8,128)S(1)}, u32[]{:S(2)}, u32[]{:S(2)}) %collective-permute-start.8) | collective-permute-done | bytes 1048608 | tf_op jit(solution)/shard_map/ppermute | solution.py:39
  319.2 0.8 fusion.4
  320.1 1.8 fusion.3
  321.9 1.3 collective-permute-start.9
  323.4 15.6 %collective-permute-done.9 = f32[256,1024]{1,0:T(8,128)} collective-permute-done((f32[256,1024]{1,0:T(8,128)}, f32[256,1024]{1,0:T(8,128)}, u32[]{:S(2)}, u32[]{:S(2)}) %collective-permute-start.9) | collective-permute-done | bytes 1048608 | tf_op jit(solution)/shard_map/ppermute | solution.py:39
  339.1 2.7 fusion.71
  342.3 2.3 fusion.42
  344.6 1.5 collective-permute-start.10
  346.2 10.1 %collective-permute-done.11 = bf16[1,256,1024]{2,1,0:T(8,128)(2,1)S(1)} collective-permute-done((bf16[1,256,1024]{2,1,0:T(8,128)(2,1)}, bf16[1,256,1024]{2,1,0:T(8,128)(2,1)S(1)}, u32[]{:S(2)}, u32[]{:S(2)}) %collective-permute-start.11) | collective-permute-done | bytes 524320 | tf_op jit(solution)/shard_map/ppermute | solution.py:25
  356.3 1.1 pad_maximum_fusion.3
  357.4 16.0 %collective-permute-done.10 = bf16[1,256,1024]{2,1,0:T(8,128)(2,1)S(1)} collective-permute-done((bf16[1,256,1024]{2,1,0:T(8,128)(2,1)S(1)}, bf16[1,256,1024]{2,1,0:T(8,128)(2,1)S(1)}, u32[]{:S(2)}, u32[]{:S(2)}) %collective-permute-start.10) | collective-permute-done | bytes 524320 | tf_op jit(solution)/shard_map/ppermute | solution.py:25
  373.8 3.1 multiply_bitcast_fusion
  376.9 1.2 reverse_select_fusion.1
  378.2 12.8 %all-gather.15.cloned.1.call-done = bf16[512,1024]{1,0:T(8,128)(2,1)} async-done(((bf16[256,1024]{1,0:T(8,128)(2,1)}), bf16[512,1024]{1,0:T(8,128)(2,1)}) %all-gather.15.cloned.1.call-update) | async-done | bytes 1048592 | tf_op jit(solution)/shard_map/all_gather | solution.py:107
  390.9 2.3 multiply_bitcast_fusion.1
  393.6 6.5 %multiply_subtract_fusion = (f32[2,512,1024]{2,1,0:T(8,128)}, f32[2,512,1024]{2,1,0:T(8,128)}) fusion(f32[2,512,1024]{2,1,0:T(8,128)S(1)} %copy-done.8, f32[1,512,1024]{2,1,0:T(8,128)S(1)} %copy-done.13, f32[1,512,1024]{2,1,0:T(8,128)} %copy-done.14, f32[2,512,1024]{2,1,0:T(8,128)} %param.6, f32[1,512,1024]{2,1,0:T(8,128)} %multiply_bitcast_fusion, ...), kind=kLoop, calls=%fused_computation.2 | loop fusion | flops 10485760 | bytes 25165824 | tf_op jit(solution)/shard_map/sub | solution.py:119
  (61 shorter events, 6.1 us)
Async XLA Ops:
  7.2 63.6 %copy-start.17 = (f32[1,256,1024]{2,1,0:T(8,128)S(1)}, f32[1,256,1024]{2,1,0:T(8,128)}, u32[]{:S(2)}) copy-start(f32[1,256,1024]{2,1,0:T(8,128)} %param.7) | copy-start | bytes 3145732
  7.2 63.6 %all-gather.7.cloned.1.call-start = ((), (), s32[]{:S(2)}) async-start(), calls=%async_computation | async-start | bytes 6291456 | tf_op jit(solution)/shard_map/all_gather | solution.py:89
  11.2 173.4 %all-gather.11.cloned.1.call-start = ((), (), s32[]{:S(2)}) async-start(), calls=%async_computation.2 | async-start | bytes 1572864 | tf_op jit(solution)/shard_map/all_gather | solution.py:107
  70.8 2.8 copy-start
  74.3 3.9 collective-permute-start
  76.0 5.0 %copy-start.1 = (bf16[2,1024,1024]{2,1,0:T(8,128)(2,1)S(1)}, bf16[2,1024,1024]{2,1,0:T(8,128)(2,1)}, u32[]{:S(2)}) copy-start(bf16[2,1024,1024]{2,1,0:T(8,128)(2,1)} %all-gather.7.cloned.1.call-done) | copy-start | bytes 12582916
  78.2 3.6 copy-start.19
  81.7 15.5 %collective-permute-start.1 = (f32[256,1024]{1,0:T(8,128)S(1)}, f32[256,1024]{1,0:T(8,128)S(1)}, u32[]{:S(2)}, u32[]{:S(2)}) collective-permute-start(f32[256,1024]{1,0:T(8,128)S(1)} %fusion.31), channel_id=1, source_target_pairs={{0,2},{2,4},{4,6},{6,8},{8,10},{10,12},{12,14},{14,16},{16,18},{18... | collective-permute-start | bytes 3145736 | tf_op jit(solution)/shard_map/ppermute | solution.py:39
  97.6 3.3 copy-start.15
  101.0 3.3 copy-start.2
  101.0 3.6 copy-start.18
  104.0 3.1 copy-start.11
  107.1 17.6 %collective-permute-start.2 = (f32[256,1024]{1,0:T(8,128)}, f32[256,1024]{1,0:T(8,128)}, u32[]{:S(2)}, u32[]{:S(2)}) collective-permute-start(f32[256,1024]{1,0:T(8,128)} %fusion.25), channel_id=1, source_target_pairs={{2,0},{4,2},{6,4},{8,6},{10,8},{12,10},{14,12},{16,14},{18,16},{20... | collective-permute-start | bytes 3145736 | tf_op jit(solution)/shard_map/ppermute | solution.py:39
  108.4 19.5 %copy-start.3 = (bf16[2,1024,1024]{2,1,0:T(8,128)(2,1)S(1)}, bf16[2,1024,1024]{2,1,0:T(8,128)(2,1)}, u32[]{:S(2)}) copy-start(bf16[2,1024,1024]{2,1,0:T(8,128)(2,1)} %all-gather.7.cloned.1.call-done) | copy-start | bytes 12582916
  129.7 17.2 %collective-permute-start.3 = (f32[256,1024]{1,0:T(8,128)}, f32[256,1024]{1,0:T(8,128)}, u32[]{:S(2)}, u32[]{:S(2)}) collective-permute-start(f32[256,1024]{1,0:T(8,128)} %fusion.23), channel_id=1, source_target_pairs={{2,0},{4,2},{6,4},{8,6},{10,8},{12,10},{14,12},{16,14},{18,16},{20... | collective-permute-start | bytes 3145736 | tf_op jit(solution)/shard_map/ppermute | solution.py:39
  131.0 68.7 %all-gather.9.cloned.1.call-start = ((), (), s32[]{:S(2)}) async-start(), calls=%async_computation.1 | async-start | bytes 1572864 | tf_op jit(solution)/shard_map/all_gather | solution.py:107
  149.5 14.6 %collective-permute-start.5 = (bf16[1,256,1024]{2,1,0:T(8,128)(2,1)}, bf16[1,256,1024]{2,1,0:T(8,128)(2,1)}, u32[]{:S(2)}, u32[]{:S(2)}) collective-permute-start(bf16[1,256,1024]{2,1,0:T(8,128)(2,1)} %bitcast.11), channel_id=1, source_target_pairs={{0,1},{1,0},{2,3},{3,2},{4,5},{5,4},{6,7},{7,6},{8,9},{9,8},{10,11... | collective-permute-start | bytes 1572872 | tf_op jit(solution)/shard_map/ppermute | solution.py:25
  153.8 27.4 %collective-permute-start.4 = (bf16[1,256,1024]{2,1,0:T(8,128)(2,1)}, bf16[1,256,1024]{2,1,0:T(8,128)(2,1)S(1)}, u32[]{:S(2)}, u32[]{:S(2)}) collective-permute-start(bf16[1,256,1024]{2,1,0:T(8,128)(2,1)} %bitcast.6), channel_id=1, source_target_pairs={{0,1},{1,0},{2,3},{3,2},{4,5},{5,4},{6,7},{7,6},{8,9},{9,8},{10,11... | collective-permute-start | bytes 1572872 | tf_op jit(solution)/shard_map/ppermute | solution.py:25
  155.2 111.7 %all-gather.13.cloned.1.call-start = ((), (), s32[]{:S(2)}) async-start(), calls=%async_computation.3 | async-start | bytes 6291456 | tf_op jit(solution)/shard_map/all_gather | solution.py:89
  181.2 0.8 copy-start.20
  199.6 3.6 copy-start.7
  201.9 1.4 copy-start.14
  203.3 63.7 %copy-start.16 = (bf16[256,1024]{1,0:T(8,128)(2,1)S(1)}, bf16[256,1024]{1,0:T(8,128)(2,1)}, u32[]{:S(2)}) copy-start(bf16[256,1024]{1,0:T(8,128)(2,1)} %copy-done.15) | copy-start | bytes 1572868
  209.1 164.7 %all-gather.17.cloned.1.call-start = ((), (), s32[]{:S(2)}) async-start(), calls=%async_computation.5 | async-start | bytes 1572864 | tf_op jit(solution)/shard_map/all_gather | solution.py:107
  266.9 2.8 copy-start.4
  270.5 3.9 collective-permute-start.6
  276.0 15.6 %collective-permute-start.7 = (f32[256,1024]{1,0:T(8,128)S(1)}, f32[256,1024]{1,0:T(8,128)S(1)}, u32[]{:S(2)}, u32[]{:S(2)}) collective-permute-start(f32[256,1024]{1,0:T(8,128)S(1)} %fusion.11), channel_id=1, source_target_pairs={{0,2},{2,4},{4,6},{6,8},{8,10},{10,12},{12,14},{14,16},{16,18},{18... | collective-permute-start | bytes 3145736 | tf_op jit(solution)/shard_map/ppermute | solution.py:39
  292.7 3.7 copy-start.12
  296.3 3.6 copy-start.5
  299.7 19.6 %copy-start.9 = (f32[256,1024]{1,0:T(8,128)}, f32[256,1024]{1,0:T(8,128)S(1)}, u32[]{:S(2)}) copy-start(f32[256,1024]{1,0:T(8,128)S(1)} %get-tuple-element.19) | copy-start | bytes 3145732
  303.2 16.0 %collective-permute-start.8 = (f32[256,1024]{1,0:T(8,128)S(1)}, f32[256,1024]{1,0:T(8,128)S(1)}, u32[]{:S(2)}, u32[]{:S(2)}) collective-permute-start(f32[256,1024]{1,0:T(8,128)S(1)} %fusion.5), channel_id=1, source_target_pairs={{2,0},{4,2},{6,4},{8,6},{10,8},{12,10},{14,12},{16,14},{18,16},{20... | collective-permute-start | bytes 3145736 | tf_op jit(solution)/shard_map/ppermute | solution.py:39
  320.1 19.0 %copy-start.10 = (f32[256,1024]{1,0:T(8,128)S(1)}, f32[256,1024]{1,0:T(8,128)}, u32[]{:S(2)}) copy-start(f32[256,1024]{1,0:T(8,128)} %copy-done.9) | copy-start | bytes 3145732
  321.9 17.2 %collective-permute-start.9 = (f32[256,1024]{1,0:T(8,128)}, f32[256,1024]{1,0:T(8,128)}, u32[]{:S(2)}, u32[]{:S(2)}) collective-permute-start(f32[256,1024]{1,0:T(8,128)} %fusion.3), channel_id=1, source_target_pairs={{2,0},{4,2},{6,4},{8,6},{10,8},{12,10},{14,12},{16,14},{18,16},{20... | collective-permute-start | bytes 3145736 | tf_op jit(solution)/shard_map/ppermute | solution.py:39
  323.2 67.8 %all-gather.15.cloned.1.call-start = ((), (), s32[]{:S(2)}) async-start(), calls=%async_computation.4 | async-start | bytes 1572864 | tf_op jit(solution)/shard_map/all_gather | solution.py:107
  323.4 18.9 %copy-start.6 = (bf16[2,1024,1024]{2,1,0:T(8,128)(2,1)S(1)}, bf16[2,1024,1024]{2,1,0:T(8,128)(2,1)}, u32[]{:S(2)}) copy-start(bf16[2,1024,1024]{2,1,0:T(8,128)(2,1)} %all-gather.13.cloned.1.call-done) | copy-start | bytes 12582916
  341.8 14.5 %collective-permute-start.11 = (bf16[1,256,1024]{2,1,0:T(8,128)(2,1)}, bf16[1,256,1024]{2,1,0:T(8,128)(2,1)S(1)}, u32[]{:S(2)}, u32[]{:S(2)}) collective-permute-start(bf16[1,256,1024]{2,1,0:T(8,128)(2,1)} %bitcast.23), channel_id=1, source_target_pairs={{0,1},{1,0},{2,3},{3,2},{4,5},{5,4},{6,7},{7,6},{8,9},{9,8},{10,11... | collective-permute-start | bytes 1572872 | tf_op jit(solution)/shard_map/ppermute | solution.py:25
  344.6 28.8 %collective-permute-start.10 = (bf16[1,256,1024]{2,1,0:T(8,128)(2,1)S(1)}, bf16[1,256,1024]{2,1,0:T(8,128)(2,1)S(1)}, u32[]{:S(2)}, u32[]{:S(2)}) collective-permute-start(bf16[1,256,1024]{2,1,0:T(8,128)(2,1)S(1)} %bitcast.98), channel_id=1, source_target_pairs={{0,1},{1,0},{2,3},{3,2},{4,5},{5,4},{6,7},{7,6},{8,9},{9,8},{10,11... | collective-permute-start | bytes 1572872 | tf_op jit(solution)/shard_map/ppermute | solution.py:25
  376.9 16.3 %copy-start.13 = (f32[1,512,1024]{2,1,0:T(8,128)S(1)}, f32[1,512,1024]{2,1,0:T(8,128)}, u32[]{:S(2)}) copy-start(f32[1,512,1024]{2,1,0:T(8,128)} %multiply_bitcast_fusion.2) | copy-start | bytes 6291460
  390.9 2.7 copy-start.8
Sparse Core Ops, SparseCore 0:
  11.3 59.4 all-gather.6
  131.1 45.2 all-gather.10
  178.0 21.6 all-gather.8
  209.2 57.6 all-gather.12
  323.3 45.3 all-gather.16
  370.0 20.8 all-gather.14
